TPU v7x, 32 devices: a whole 2x2x4 slice. The times are simulated.
32 devices in a mesh: groups: 2 (over y), fsdp: 8 (over z, x), blk: 2 (over core).
Axes of the slice: x: 2, y: 2, z: 4, core: 2. Of those that a mesh axis runs over, the one named last changes fastest.
Arguments:
- block_input: bfloat16 [8192, 5120], P(('groups', 'fsdp', 'blk')), parts along dimension 0, may hold values from -3 to 3
- gate: float32 [10240], P('groups'), parts along dimension 0, may hold values from -6 to 6
- q_fresh: bfloat16 [8192, 2560], P(('groups', 'fsdp', 'blk')), parts along dimension 0, may hold values from -48.5 to 48.5
- kv_fresh: bfloat16 [8192, 2, 2560], P(('groups', 'fsdp', 'blk')), parts along dimension 0, may hold values from -6 to 6
- kv_cache: bfloat16 [8192, 2, 2560], P(('groups', 'fsdp', 'blk')), parts along dimension 0, may hold values from -6 to 6
- active_list: int32 [16, 2, 2], P(('groups', 'fsdp')), parts along dimension 0, may hold values from 0 to 1, as said below
- active_count: int32 [16, 2], P(('groups', 'fsdp')), parts along dimension 0, may hold values from 0 to 2, as said below
- key_list: int32 [16, 4, 3], P(('groups', 'fsdp')), parts along dimension 0, may hold values from 0 to 3, as said below
- out_weight: bfloat16 [2560, 5120], P('fsdp'), may hold values from -0.125 to 0.125
Outputs:
- block_output: bfloat16 [8192, 5120], P(('groups', 'fsdp', 'blk')), parts along dimension 0
There are 2 independent parts, one for each index of `groups`. A program takes and returns all parts, laid end to end along the dimension named above; an argument that names none is the same for every part. Nothing has to cross between parts.
Inputs may be any that keep to these rules, and one draw needn't show every extreme that they name: `active_list`: each row [f, b] holds every tile number once; its first active_count[f, b] entries are the active tiles. `active_count`: some token block has all 2 tiles active. `key_list`: entry [f, g] holds 3 different tile ids of group f, the first one being g.
All inputs are finite; a program needn't handle non-finite values.
Results may differ from a plain program's by a relative error of at most 0.0034.
Values may be sent and summed in bfloat16 or wider, within the bound.
A program may use at most 128 MiB of HBM per device.

v0:
```python
import math

import jax
import jax.numpy as jnp
from jax import lax
from jax.sharding import PartitionSpec as P

HEADS = 20
HEAD_DIM = 128


MASKED = -1e30


def swapped(block, axis, apart):
    count = lax.axis_size(axis)
    route = []
    for low in range(count):
        high = low | 1 << apart
        if high != low and high < count:
            route += [(low, high), (high, low)]
    return lax.ppermute(block, axis, route)


def tile_flags(tile_list, tile_count):
    slot_ids = jnp.arange(tile_list.shape[0], dtype=jnp.int32)
    listed = (tile_list[:, None] == slot_ids[None, :]) & (slot_ids[:, None] < tile_count)
    return jnp.any(listed, axis=0)


def block_partial(query_tile, key_rows, value_rows, allowed):
    tile_rows = query_tile.shape[0]
    query3 = query_tile.reshape(tile_rows, HEADS, HEAD_DIM)
    key3 = key_rows.reshape(key_rows.shape[0], HEADS, HEAD_DIM)
    value3 = value_rows.reshape(value_rows.shape[0], HEADS, HEAD_DIM)
    scores = jnp.einsum(
        "qhd,khd->hqk", query3, key3, preferred_element_type=jnp.float32
    ) / math.sqrt(HEAD_DIM)
    scores = jnp.where(allowed[None, None, :], scores, MASKED)
    row_max = jnp.max(scores, axis=2)
    exp_terms = jnp.where(allowed[None, None, :], jnp.exp(scores - row_max[:, :, None]), 0.0)
    row_total = jnp.sum(exp_terms, axis=2)
    weights = exp_terms.astype(jnp.bfloat16)
    block_out = jnp.einsum("hqk,khd->hqd", weights, value3, preferred_element_type=jnp.float32)
    return (block_out, row_max, row_total)


def attend_block(
    queries, tile_list, tile_count, query_side, key_rows, value_rows, key_side, key_table
):
    tiles_dev = tile_list.shape[0]
    tile_rows = queries.shape[0] // tiles_dev
    slot_ids = jnp.arange(tiles_dev, dtype=jnp.int32)
    key_tiles = key_side * tiles_dev + slot_ids
    init_state = (
        jnp.zeros((tiles_dev, HEADS, tile_rows, HEAD_DIM), jnp.float32),
        jnp.full((tiles_dev, HEADS, tile_rows), MASKED, jnp.float32),
        jnp.zeros((tiles_dev, HEADS, tile_rows), jnp.float32),
    )

    def one_slot(slot_idx, carry_state):
        tile_pos = tile_list[slot_idx]
        query_tile = lax.dynamic_slice_in_dim(queries, tile_pos * tile_rows, tile_rows, 0)
        listed = key_table[query_side * tiles_dev + tile_pos]
        allowed_tiles = jnp.any(key_tiles[:, None] == listed[None, :], axis=1)
        allowed = jnp.repeat(allowed_tiles, tile_rows, total_repeat_length=tiles_dev * tile_rows)
        partial_value = block_partial(query_tile, key_rows, value_rows, allowed)
        return tuple(
            (whole.at[tile_pos].set(piece) for whole, piece in zip(carry_state, partial_value))
        )

    return lax.fori_loop(0, tile_count, one_slot, init_state)


def merge_states(earlier, later_state):
    out_one, max_one, total_one = earlier
    out_two, max_two, total_two = later_state
    joint_max = jnp.maximum(max_one, max_two)
    scale_one = jnp.exp(max_one - joint_max)
    scale_two = jnp.exp(max_two - joint_max)
    summed = out_one * scale_one[..., None] + out_two * scale_two[..., None]
    return (summed, total_one * scale_one + total_two * scale_two)


def local(
    block_input, gate, q_fresh, kv_fresh, kv_cache, active_list, active_count, key_list, out_weight
):
    own_side = lax.axis_index("blk")
    other_side = 1 - own_side
    tiles_dev = active_list.shape[2]
    tok_dev = block_input.shape[0]
    tile_rows = tok_dev // tiles_dev
    own_list = active_list[0, own_side]
    own_count = active_count[0, own_side]
    flags = tile_flags(own_list, own_count)
    row_flags = jnp.repeat(flags, tile_rows, total_repeat_length=tok_dev)
    resident = jnp.where(row_flags[:, None, None], kv_fresh, kv_cache)
    key_table = key_list[0]
    own_state = attend_block(
        q_fresh, own_list, own_count, own_side, resident[:, 0], resident[:, 1], own_side, key_table
    )
    other_kv = swapped(resident, "blk", 0)
    other_state = attend_block(
        q_fresh,
        own_list,
        own_count,
        own_side,
        other_kv[:, 0],
        other_kv[:, 1],
        other_side,
        key_table,
    )
    summed, denom = merge_states(own_state, other_state)
    denom = jnp.where(flags[:, None, None], denom, 1.0)
    attended = (
        (summed / denom[..., None])
        .transpose(0, 2, 1, 3)
        .reshape(tok_dev, HEADS * HEAD_DIM)
        .astype(jnp.bfloat16)
    )
    half_cols = out_weight.shape[1] // 2
    own_cols = lax.dynamic_slice_in_dim(out_weight, own_side * half_cols, half_cols, 1)
    half_weight = lax.all_gather(own_cols, "fsdp", axis=0, tiled=True)
    partner_rows = swapped(attended, "blk", 0)
    own_part = jnp.dot(attended, half_weight, preferred_element_type=jnp.float32)
    partner_part = jnp.dot(partner_rows, half_weight, preferred_element_type=jnp.float32)
    returned = swapped(partner_part, "blk", 0)
    projected = jnp.where(
        own_side == 0,
        jnp.concatenate([own_part, returned], axis=1),
        jnp.concatenate([returned, own_part], axis=1),
    )
    mixed = block_input.astype(jnp.float32) + gate[None, :] * projected
    return jnp.where(row_flags[:, None], mixed.astype(jnp.bfloat16), block_input)


def solution(mesh):
    in_specs = (
        P(("groups", "fsdp", "blk"), None),
        P("groups"),
        P(("groups", "fsdp", "blk"), None),
        P(("groups", "fsdp", "blk"), None, None),
        P(("groups", "fsdp", "blk"), None, None),
        P(("groups", "fsdp"), None, None),
        P(("groups", "fsdp"), None),
        P(("groups", "fsdp"), None, None),
        P("fsdp", None),
    )
    out_specs = P(("groups", "fsdp", "blk"), None)
    return jax.shard_map(local, mesh=mesh, in_specs=in_specs, out_specs=out_specs, check_vma=False)
```

profile of v0, /device:TPU:0, one launch (start us, length us, event | category | flops | bytes accessed | tf_op | source)
XLA Modules:
  0.0 244.2 jit_solution(7101395316258449989)
XLA Ops:
  6.5 0.0 copy-start
  6.5 0.0 all-gather.2.cloned.1.call-start
  6.6 1.5 constant_dynamic-slice_fusion.5
  8.0 0.7 iota_compare_fusion
  8.7 0.7 fusion.47
  9.4 0.1 and_reduce_fusion.4
  9.5 0.6 fusion.55
  10.1 1.4 select_reduce_fusion
  11.5 7.3 %copy.34 = bf16[256,2,2560]{0,2,1:T(8,128)(2,1)} copy(bf16[256,2,2560]{2,1,0:T(2,128)(2,1)} %param.36) | data formatting | bytes 5242880 | tf_op args[3]
  18.8 7.3 %copy.35 = bf16[256,2,2560]{0,2,1:T(8,128)(2,1)} copy(bf16[256,2,2560]{2,1,0:T(2,128)(2,1)} %param.37) | data formatting | bytes 5242880 | tf_op args[4]
  26.1 4.3 %broadcast_select_fusion = bf16[256,2,2560]{0,2,1:T(8,128)(2,1)} fusion(bf16[256,2,2560]{0,2,1:T(8,128)(2,1)} %copy.34, bf16[256,2,2560]{0,2,1:T(8,128)(2,1)} %copy.35, pred[256]{0:T(512)(128)(4,1)S(1)} %and_select_fusion), kind=kLoop, calls=%fused_computation.64 | loop fusion | flops 1310720 | bytes 7864576 | tf_op jit(solution)/shard_map/jit(_where)/select_n | solution.py:97
  30.4 0.5 collective-permute-start
  30.9 1.3 constant_dynamic-slice_fusion.4
  32.2 0.0 all-gather.2.cloned.1.call-update
  32.2 2.4 copy.36
  34.7 0.0 copy-done.6
  34.7 0.1 copy.33
  34.8 3.4 %fusion.53 = (bf16[256,1,2560]{0,2,1:T(8,128)(2,1)}, bf16[256,1,2560]{0,2,1:T(8,128)(2,1)}) fusion(bf16[256,2,2560]{0,2,1:T(8,128)(2,1)} %broadcast_select_fusion), kind=kLoop, calls=%fused_computation.88 | loop fusion | bytes 5242880 | tf_op jit(solution)/shard_map/slice | solution.py:100
  38.2 1.8 broadcast.442.clone.1
  40.0 0.0 copy-done.3
  40.0 0.0 copy-done.4
  40.0 18.6 %while.47 = (s32[]{:T(128)}, f32[2,20,128,128]{3,2,1,0:T(8,128)}, f32[2,20,128]{2,1,0:T(8,128)S(1)}, f32[2,20,128]{2,1,0:T(8,128)S(1)}, s32[]{:T(128)}, /*index=...) while((s32[]{:T(128)}, f32[2,20,128,128]{3,2,1,0:T(8,128)}, ...), condition=%wide.region_7.9_spmd.clone.clone, body=%wide.region_1.8_spmd.clone.clone.sunk | while | flops 344394592 | bytes 15190492 | solution.py:72
  40.7 0.7 dynamic_slice.87
  42.1 0.2 compare_reduce_fusion.5
  42.2 0.7 fusion.98
  42.9 1.2 select_select_fusion.5
  44.8 1.2 constant_dynamic-slice_fusion.10
  46.1 2.0 fusion.99
  48.1 1.2 fusion.100
  51.3 0.8 and_reduce_fusion.12
  52.1 0.7 fusion.101
  52.8 0.8 and_reduce_fusion.11
  53.6 4.2 %select_dynamic-update-slice_fusion.5 = f32[2,20,128,128]{3,2,1,0:T(8,128)} fusion(f32[2,20,128,128]{3,2,1,0:T(8,128)} %get-tuple-element.974, s32[]{:T(128)} %select_n.324, bf16[256,20,128]{0,2,1:T(8,128)(2,1)} %bitcast.138, f32[20,128,256]{2,1,0:T(8,128)S(1)} %get-tuple-element.886, f32[20,128]{1,0:T(8,128)S(1)} %get-tuple-element.887, ...), kind=kOutput, calls=%fused_computation.36.clone.1 | convolution fusion | flops 171376640 | bytes 6565120 | tf_op jit(solution)/shard_map/while/body/hqk,khd->hqd/dot_general | solution.py:44
  58.6 0.0 collective-permute-done
  58.6 3.4 %fusion.54 = (bf16[256,1,2560]{0,2,1:T(8,128)(2,1)}, bf16[256,1,2560]{0,2,1:T(8,128)(2,1)}) fusion(bf16[256,2,2560]{0,2,1:T(8,128)(2,1)} %collective-permute-done), kind=kLoop, calls=%fused_computation.89 | loop fusion | bytes 5242880 | tf_op jit(solution)/shard_map/slice | solution.py:109
  62.0 1.8 broadcast.442.clone
  63.8 17.8 %while.46 = (s32[]{:T(128)}, f32[2,20,128,128]{3,2,1,0:T(8,128)}, f32[2,20,128]{2,1,0:T(8,128)S(1)}, f32[2,20,128]{2,1,0:T(8,128)S(1)}, s32[]{:T(128)}, /*index=...) while((s32[]{:T(128)}, f32[2,20,128,128]{3,2,1,0:T(8,128)}, ...), condition=%wide.region_14.16_spmd.clone, body=%wide.region_8.15_spmd.clone.sunk | while | flops 344394592 | bytes 15190500 | solution.py:72
  64.5 0.6 dynamic_slice.84
  65.8 0.2 compare_reduce_fusion.4
  65.9 0.6 fusion.89
  66.5 1.2 select_select_fusion.4
  68.4 1.1 constant_dynamic-slice_fusion.9
  69.5 2.0 fusion.90
  71.5 1.2 fusion.91
  74.5 0.7 and_reduce_fusion.10
  75.3 0.6 fusion.92
  75.9 0.7 and_reduce_fusion.9
  76.6 4.1 %select_dynamic-update-slice_fusion.4 = f32[2,20,128,128]{3,2,1,0:T(8,128)} fusion(f32[2,20,128,128]{3,2,1,0:T(8,128)} %get-tuple-element.912, s32[]{:T(128)} %select_n.313, bf16[256,20,128]{0,2,1:T(8,128)(2,1)} %bitcast.137, f32[20,128,256]{2,1,0:T(8,128)S(1)} %get-tuple-element.869, f32[20,128]{1,0:T(8,128)S(1)} %get-tuple-element.870, ...), kind=kOutput, calls=%fused_computation.8.clone.1 | convolution fusion | flops 171376640 | bytes 6565120 | tf_op jit(solution)/shard_map/while/body/hqk,khd->hqd/dot_general | solution.py:44
  81.6 0.1 add_select_fusion
  81.7 5.1 %fusion.42 = bf16[2,128,20,128]{3,1,2,0:T(8,128)(2,1)S(1)} fusion(f32[2,20,128]{2,1,0:T(8,128)S(1)} %get-tuple-element.703, f32[2,20,128,128]{3,2,1,0:T(8,128)} %get-tuple-element.525, f32[2,20,128]{2,1,0:T(8,128)S(1)} %get-tuple-element.705, f32[2,20,128,128]{3,2,1,0:T(8,128)} %get-tuple-element.522, f32[2,20,128]{2,1,0:T(8,128)S(1)} %get-tuple-element.704), kind=kLoop, calls=%fused_computation.66 | loop fusion | flops 3276800 | bytes 6615040 | tf_op jit(solution)/shard_map/convert_element_type | solution.py:119
  86.8 1.0 copy.38
  87.8 0.2 copy.48
  88.0 0.1 collective-permute-start.1
  88.1 3.0 %collective-permute-done.1 = bf16[256,2560]{0,1:T(8,128)(2,1)S(1)} collective-permute-done((bf16[256,2560]{0,1:T(8,128)(2,1)S(1)}, bf16[256,2560]{0,1:T(8,128)(2,1)S(1)}, u32[]{:S(2)}, u32[]{:S(2)}) %collective-permute-start.1) | collective-permute-done | bytes 1310752 | tf_op jit(solution)/shard_map/ppermute | solution.py:22
  91.1 126.2 %all-gather.2.cloned.1.call-done = bf16[2560,2560]{1,0:T(8,128)(2,1)} async-done(((bf16[320,2560]{1,0:T(8,128)(2,1)}), bf16[2560,2560]{1,0:T(8,128)(2,1)}) %all-gather.2.cloned.1.call-update) | async-done | bytes 13107216 | tf_op jit(solution)/shard_map/all_gather | solution.py:123
  217.3 8.1 %fusion.56 = f32[256,2560]{1,0:T(8,128)} fusion(bf16[256,2560]{0,1:T(8,128)(2,1)S(1)} %collective-permute-done.1, bf16[2560,2560]{1,0:T(8,128)(2,1)} %all-gather.2.cloned.1.call-done), kind=kOutput, calls=%fused_computation.91 | convolution fusion | flops 3355443200 | bytes 17039360 | tf_op jit(solution)/shard_map/dot_general | solution.py:126
  225.4 0.0 collective-permute-start.2
  225.5 6.8 %fusion.48 = f32[256,2560]{1,0:T(8,128)S(1)} fusion(bf16[2560,2560]{1,0:T(8,128)(2,1)} %all-gather.2.cloned.1.call-done, bf16[320,8,2,128]{3,2,1,0:T(2,128)(2,1)S(1)} %bitcast.136), kind=kOutput, calls=%fused_computation.85 | convolution fusion | flops 3355443200 | bytes 17039360 | tf_op jit(solution)/shard_map/dot_general | solution.py:125
  232.3 0.0 collective-permute-done.2
  232.3 0.0 copy-done.2
  232.3 0.0 copy-done.5
  232.3 0.0 copy-start.1
  232.3 5.0 %fusion.41 = bf16[256,5120]{1,0:T(8,128)(2,1)} fusion(bf16[256,5120]{1,0:T(8,128)(2,1)S(1)} %copy-done.2, f32[256,2560]{1,0:T(8,128)S(1)} %fusion.48, f32[256,2560]{1,0:T(8,128)} %collective-permute-done.2, f32[5120]{0:T(1024)S(1)} %copy-done.5, pred[256]{0:T(512)(128)(4,1)S(1)} %and_select_fusion, pred[]{:T(512)S(6)} %eq.84), kind=kLoop, calls=%fused_computation.62 | loop fusion | flops 10485760 | bytes 10506497 | tf_op jit(solution)/shard_map/jit(_where)/select_n | solution.py:134
  237.3 0.0 copy-done.1
  (17 shorter events, 0.1 us)
Async XLA Ops:
  6.5 24.4 %copy-start = (bf16[320,5120]{1,0:T(8,128)(2,1)S(1)}, bf16[320,5120]{1,0:T(8,128)(2,1)}, u32[]{:S(2)}) copy-start(bf16[320,5120]{1,0:T(8,128)(2,1)} %param.41) | copy-start | bytes 9830404
  6.5 210.8 %all-gather.2.cloned.1.call-start = ((), (), s32[]{:S(2)}) async-start(), calls=%async_computation | async-start | bytes 14745600 | tf_op jit(solution)/shard_map/all_gather | solution.py:123
  30.4 28.1 %collective-permute-start = (bf16[256,2,2560]{0,2,1:T(8,128)(2,1)}, bf16[256,2,2560]{0,2,1:T(8,128)(2,1)}, u32[]{:S(2)}, u32[]{:S(2)}) collective-permute-start(bf16[256,2,2560]{0,2,1:T(8,128)(2,1)} %broadcast_select_fusion), channel_id=1, source_target_pairs={{0,1},{1,0},{2,3},{3,2},{4,5},{5,4},{6,7},{7,6},{8,9},{9,8},{10,11... | collective-permute-start | bytes 7864328 | tf_op jit(solution)/shard_map/ppermute | solution.py:22
  32.2 2.5 %copy-start.6 = (s32[1,4,3]{1,0,2:T(1,128)S(1)}, s32[1,4,3]{1,0,2:T(1,128)}, u32[]{:S(2)}) copy-start(s32[1,4,3]{1,0,2:T(1,128)} %param.40) | copy-start | bytes 148
  38.2 1.8 copy-start.3
  38.2 1.8 copy-start.4
  88.0 3.1 %collective-permute-start.1 = (bf16[256,2560]{0,1:T(8,128)(2,1)S(1)}, bf16[256,2560]{0,1:T(8,128)(2,1)S(1)}, u32[]{:S(2)}, u32[]{:S(2)}) collective-permute-start(bf16[256,2560]{0,1:T(8,128)(2,1)S(1)} %bitcast.139), channel_id=1, source_target_pairs={{0,1},{1,0},{2,3},{3,2},{4,5},{5,4},{6,7},{7,6},{8,9},{9,8},{10,11... | collective-permute-start | bytes 3932168 | tf_op jit(solution)/shard_map/ppermute | solution.py:22
  225.4 6.9 %collective-permute-start.2 = (f32[256,2560]{1,0:T(8,128)}, f32[256,2560]{1,0:T(8,128)}, u32[]{:S(2)}, u32[]{:S(2)}) collective-permute-start(f32[256,2560]{1,0:T(8,128)} %fusion.56), channel_id=1, source_target_pairs={{0,1},{1,0},{2,3},{3,2},{4,5},{5,4},{6,7},{7,6},{8,9},{9,8},{10,11... | collective-permute-start | bytes 7864328 | tf_op jit(solution)/shard_map/ppermute | solution.py:22
  225.4 6.9 %copy-start.2 = (bf16[256,5120]{1,0:T(8,128)(2,1)S(1)}, bf16[256,5120]{1,0:T(8,128)(2,1)}, u32[]{:S(2)}) copy-start(bf16[256,5120]{1,0:T(8,128)(2,1)} %param.33) | copy-start | bytes 7864324
  225.4 6.9 %copy-start.5 = (f32[5120]{0:T(1024)S(1)}, f32[5120]{0:T(1024)}, u32[]{:S(2)}) copy-start(f32[5120]{0:T(1024)} %param.34) | copy-start | bytes 61444
  232.3 5.0 %copy-start.1 = (bf16[320,5120]{1,0:T(8,128)(2,1)S(1)}, bf16[320,5120]{1,0:T(8,128)(2,1)}, u32[]{:S(2)}) copy-start(bf16[320,5120]{1,0:T(8,128)(2,1)} %param.41) | copy-start | bytes 9830404
Sparse Core Ops, SparseCore 0:
  32.4 184.8 all-gather.1
where the time goes:
time: 246 us; the launch traced here: 244 us
  waiting for transfers between devices  129 us (52%)
  local copies, waits for them, and re-layouts  37.8 us (15%)
  matrix products  27.3 us (11%)
  other arithmetic  26.2 us (11%)
  between operations  13.5 us (5%)
  loops' own time  9.54 us (4%)
    all_gather x1, waiting for transfers between devices, local(): half_weight = lax.all_gather(own_cols, 'fsdp', axis=0, tiled=True)  126 us
    unnamed x19, local copies, waits for them, and re-layouts  17.4 us
    another operation x2, loops' own time, attend_block(): return lax.fori_loop(0, tile_count, one_slot, init_state)  9.54 us
    dot_general x2, matrix products, block_partial(): jnp.einsum('hqk,khd->hqd', weights, value3, preferred_element_type=jnp.fl...  8.35 us
    dot_general x1, matrix products, local(): jnp.dot(partner_rows, half_weight, preferred_element_type=jnp.float32)  8.14 us
    dot_general x1, matrix products, local(): jnp.dot(attended, half_weight, preferred_element_type=jnp.float32)  6.85 us
    convert_element_type x1, other arithmetic, local(): attended = (summed / denom[..., None]).transpose(0, 2, 1, 3).reshape(tok_...  5.11 us
    select_n x1, other arithmetic, local(): jnp.where(row_flags[:, None], mixed.astype(jnp.bfloat16), block_input)  4.99 us
  transfers between devices with their start and end apart: 4, of which 2 were waited for; matrix products, arithmetic and copies ran while one was open for 22% of the time, Pallas kernels for 0%

commit v1 on v0

--- a/solution.py
+++ b/solution.py
@@ -1,8 +1,11 @@
+import functools
 import math
 
 import jax
 import jax.numpy as jnp
 from jax import lax
+from jax.experimental import pallas as pl
+from jax.experimental.pallas import tpu as pltpu
 from jax.sharding import PartitionSpec as P
 
 HEADS = 20
@@ -133,6 +136,399 @@
     mixed = block_input.astype(jnp.float32) + gate[None, :] * projected
     return jnp.where(row_flags[:, None], mixed.astype(jnp.bfloat16), block_input)
 
+MESH = pl.DeviceIdType.MESH
+CHUNKS = 10
+LINE = 2
+
+
+def fused(
+    depth,
+    active_list,
+    active_count,
+    key_list,
+    block_hbm,
+    gate_ref,
+    q_hbm,
+    k_hbm,
+    v_hbm,
+    w_hbm,
+    out_hbm,
+    weight,
+    queries,
+    keys,
+    values,
+    attended,
+    mixed_in,
+    mixed_out,
+    mask,
+    load_sem,
+    w_sem,
+    pair_send,
+    pair_recv,
+    send_sem,
+    recv_sem,
+    store_sem,
+    out_send,
+    out_recv,
+):
+    me = lax.axis_index("fsdp")
+    z, x = me // LINE, me % LINE
+    y = lax.axis_index("groups")
+    b = lax.axis_index("blk")
+    rows = w_hbm.shape[0]
+    tok = q_hbm.shape[0]
+    half = w_hbm.shape[1] // 2
+    width = half // CHUNKS
+    tiles = active_list.shape[2]
+    tile_rows = tok // tiles
+    heads = q_hbm.shape[1] // HEAD_DIM
+    mine = pl.multiple_of(b * half, 128)
+    theirs = pl.multiple_of((1 - b) * half, 128)
+
+    barrier = pltpu.get_barrier_semaphore()
+    targets = (
+        (z < depth - 1, {"fsdp": me + LINE}),
+        (z > 0, {"fsdp": me - LINE}),
+        (None, {"fsdp": z * LINE + 1 - x}),
+        (None, {"groups": 1 - y}),
+    )
+    core = {"blk": 1 - b}
+
+    def when(cond, body):
+        if cond is None:
+            body()
+        else:
+            pl.when(cond)(body)
+
+    def greet(device):
+        pl.semaphore_signal(barrier, inc=1, device_id=device, device_id_type=MESH)
+
+    for cond, device in targets + ((None, core),):
+        when(cond, functools.partial(greet, device))
+
+    def own_weight(c):
+        return pltpu.make_async_copy(
+            w_hbm.at[:, pl.ds(pl.multiple_of(mine + c * width, 128), width)],
+            weight.at[c, pl.ds(pl.multiple_of(me * rows, 16), rows), :],
+            w_sem.at[c],
+        )
+
+    def stream(i):
+        return jnp.where(i == 0, y, jnp.where(i < 3, 1 + 2 * y + i, 3 + i))
+
+    def passive(i):
+        return jnp.where(i == 0, 1 - y, 3 - 2 * y + i)
+
+    def every(i):
+        return jnp.where(i < 7, stream(i), passive(i - 7))
+
+    for i in range(CHUNKS):
+        own_weight(every(jnp.int32(i))).start()
+
+    loads = [
+        pltpu.make_async_copy(q_hbm, queries, load_sem.at[0]),
+        pltpu.make_async_copy(k_hbm, keys.at[pl.ds(0, tok)], load_sem.at[1]),
+        pltpu.make_async_copy(v_hbm, values.at[pl.ds(0, tok)], load_sem.at[2]),
+        pltpu.make_async_copy(
+            block_hbm.at[:, pl.ds(mine, half)], mixed_in.at[pl.ds(0, tok)], load_sem.at[3]
+        ),
+    ]
+    for load in loads:
+        load.start()
+
+    pl.semaphore_wait(barrier, 3 + (z > 0).astype(jnp.int32) + (z < depth - 1).astype(jnp.int32))
+
+    def to_core(src, dst, index):
+        return pltpu.make_async_remote_copy(
+            src_ref=src,
+            dst_ref=dst,
+            send_sem=pair_send.at[index],
+            recv_sem=pair_recv.at[index],
+            device_id=core,
+            device_id_type=MESH,
+        )
+
+    swaps = [
+        to_core(k_hbm, keys.at[pl.ds(tok, tok)], 0),
+        to_core(v_hbm, values.at[pl.ds(tok, tok)], 1),
+        to_core(block_hbm.at[:, pl.ds(theirs, half)], mixed_in.at[pl.ds(tok, tok)], 2),
+    ]
+    give = to_core(attended.at[pl.ds(0, tok)], attended.at[pl.ds(tok, tok)], 3)
+    for swap in swaps:
+        swap.start()
+
+    def shard_copy(c, s, way):
+        block = weight.at[c, pl.ds(pl.multiple_of(s * rows, 16), rows), :]
+        return pltpu.make_async_remote_copy(
+            src_ref=block,
+            dst_ref=block,
+            send_sem=send_sem.at[c, s, way],
+            recv_sem=recv_sem.at[c, s],
+            device_id=targets[way][1],
+            device_id_type=MESH,
+        )
+
+    def visit(c, first, over_y, dz, dx, done):
+        s = (z + dz) * LINE + (x if dx == 0 else 1 - x)
+        ways = []
+        if first == "z":
+            if dx == 0:
+                ways += [0] if dz <= 0 else []
+                ways += [1] if dz >= 0 else []
+                ways += [2]
+        else:
+            ways += [2] if (dz, dx) == (0, 0) else []
+            ways += [0] if dz <= 0 else []
+            ways += [1] if dz >= 0 else []
+
+        def body():
+            if (dz, dx) == (0, 0):
+                if not done:
+                    own_weight(c).wait()
+            elif not done:
+                shard_copy(c, s, 2).wait_recv()
+
+            def act(way):
+                copy = shard_copy(c, s, way)
+                if done:
+                    copy.wait_send()
+                else:
+                    copy.start()
+
+            for way in ways:
+                when(targets[way][0], functools.partial(act, way))
+            if (dz, dx) != (0, 0) and over_y is not False:
+                when(None if over_y is True else over_y, functools.partial(act, 3))
+
+        if dz < 0:
+            pl.when(z + dz >= 0)(body)
+        elif dz > 0:
+            pl.when(z + dz < depth)(body)
+        else:
+            body()
+
+    def offsets(level):
+        found = []
+        for dx in range(LINE):
+            far = level - dx
+            if 0 <= far < depth:
+                found += [(0, dx)] if far == 0 else [(-far, dx), (far, dx)]
+        return found
+
+    levels = depth + LINE - 1
+
+    def step_x(level, done=False):
+        for dz, dx in offsets(level):
+            visit(y, "x", True, dz, dx, done)
+
+    def step_z(i, level, done=False):
+        for dz, dx in offsets(level):
+            visit(stream(i), "z", i < 3, dz, dx, done)
+
+    step_x(0)
+    pl.loop(1, 7)(lambda i: step_z(i, 0))
+
+    for load in loads[:3]:
+        load.wait()
+    for swap in swaps[:2]:
+        swap.wait_recv()
+
+    for a in range(tiles):
+        for t in range(2 * tiles):
+            side = b if t < tiles else 1 - b
+            tile_id = side * tiles + t % tiles
+            listed = jnp.int32(0)
+            for slot in range(key_list.shape[2]):
+                hit = key_list[0, b * tiles + a, slot] == tile_id
+                listed = jnp.where(hit, jnp.int32(1), listed)
+            mask[pl.ds(a * tile_rows, tile_rows), pl.ds(t * tile_rows, tile_rows)] = jnp.full(
+                (tile_rows, tile_rows), listed.astype(jnp.float32), jnp.float32
+            )
+
+    def attend(h):
+        cols = pl.ds(pl.multiple_of(h * HEAD_DIM, 128), HEAD_DIM)
+        query = queries[:, cols]
+        parts = []
+        for side in range(2):
+            span = pl.ds(side * tok, tok)
+            scores = lax.dot_general(
+                query,
+                keys[span, cols],
+                (((1,), (1,)), ((), ())),
+                preferred_element_type=jnp.float32,
+            ) * (1.0 / math.sqrt(HEAD_DIM))
+            allowed = mask[:, span] > 0.5
+            scores = jnp.where(allowed, scores, MASKED)
+            top = jnp.max(scores, axis=1, keepdims=True)
+            terms = jnp.where(allowed, jnp.exp(scores - top), 0.0)
+            total = jnp.sum(terms, axis=1, keepdims=True)
+            part = jnp.dot(
+                terms.astype(jnp.bfloat16), values[span, cols], preferred_element_type=jnp.float32
+            )
+            parts.append((part, top, total))
+        (out0, max0, sum0), (out1, max1, sum1) = parts
+        joint = jnp.maximum(max0, max1)
+        scale0 = jnp.exp(max0 - joint)
+        scale1 = jnp.exp(max1 - joint)
+        denom = sum0 * scale0 + sum1 * scale1
+        result = (out0 * scale0 + out1 * scale1) / denom
+        attended[pl.ds(0, tok), cols] = result.astype(jnp.bfloat16)
+
+    def attend_range(low, high):
+        pl.loop(low, high)(attend)
+
+    each = heads // 7
+    first = heads - 6 * each
+    step_x(1)
+    attend_range(0, first)
+
+    @pl.loop(1, 7)
+    def _(i):
+        step_z(i, 1)
+        attend_range(first + (i - 1) * each, first + i * each)
+
+    give.start()
+    for level in range(2, levels - 1):
+        step_x(level)
+        pl.loop(1, 7)(functools.partial(step_z, level=level))
+
+    loads[3].wait()
+    swaps[2].wait_recv()
+    give.wait_recv()
+
+    def is_active(side, a):
+        found = jnp.int32(0)
+        for slot in range(tiles):
+            hit = (active_list[0, side, slot] == a) & (slot < active_count[0, side])
+            found = jnp.where(hit, jnp.int32(1), found)
+        return found
+
+    flags = [is_active(side, a) for side in (b, 1 - b) for a in range(tiles)]
+
+    def out_copies(c):
+        cols = pl.ds(pl.multiple_of(mine + c * width, 128), width)
+        return (
+            pltpu.make_async_copy(
+                mixed_out.at[c, pl.ds(0, tok), :], out_hbm.at[:, cols], store_sem.at[c]
+            ),
+            pltpu.make_async_remote_copy(
+                src_ref=mixed_out.at[c, pl.ds(tok, tok), :],
+                dst_ref=out_hbm.at[:, cols],
+                send_sem=out_send.at[c],
+                recv_sem=out_recv.at[c],
+                device_id=core,
+                device_id_type=MESH,
+            ),
+        )
+
+    def project(j):
+        i = jnp.where(j < 3, j, jnp.where(j < 6, j + 4, j - 3))
+        c = every(i)
+
+        @pl.when(j == 0)
+        def _():
+            step_x(levels - 1)
+
+        @pl.when((j == 1) | (j == 2) | (j >= 6))
+        def _():
+            step_z(i, levels - 1)
+
+        @pl.when((j >= 3) & (j < 6))
+        def _():
+            own_weight(c).wait()
+            for s in range(depth * LINE):
+                pl.when(me != s)(lambda s=s: shard_copy(c, s, 3).wait_recv())
+
+        projected = jnp.dot(attended[...], weight[c], preferred_element_type=jnp.float32)
+        gate = gate_ref[:, pl.ds(pl.multiple_of(mine + c * width, 128), width)]
+        cols = pl.ds(pl.multiple_of(c * width, 128), width)
+        for place, flag in enumerate(flags):
+            span = pl.ds(place * tile_rows, tile_rows)
+            before = mixed_in[span, cols].astype(jnp.float32)
+            part = projected[place * tile_rows : (place + 1) * tile_rows]
+            mixed = jnp.where(flag > 0, before + gate * part, before)
+            mixed_out[c, span, :] = mixed.astype(jnp.bfloat16)
+        for copy in out_copies(c):
+            copy.start()
+
+    pl.loop(0, CHUNKS)(project)
+
+    for swap in swaps + [give]:
+        swap.wait_send()
+    for level in range(levels):
+        step_x(level, done=True)
+        pl.loop(1, 7)(functools.partial(step_z, level=level, done=True))
+
+    @pl.loop(0, CHUNKS)
+    def _(c):
+        local_copy, remote_copy = out_copies(c)
+        local_copy.wait()
+        remote_copy.wait()
+
+
+def local_fused(
+    count, block_input, gate, q_fresh, kv_fresh, kv_cache, active_list, active_count, key_list, out_weight
+):
+    tok, width = block_input.shape
+    own_side = lax.axis_index("blk")
+    tiles = active_list.shape[2]
+    flags = tile_flags(active_list[0, own_side], active_count[0, own_side])
+    row_flags = jnp.repeat(flags, tok // tiles, total_repeat_length=tok)
+    resident = jnp.where(row_flags[:, None, None], kv_fresh, kv_cache)
+    rows = out_weight.shape[0]
+    half = width // 2
+    columns = q_fresh.shape[1]
+    smem = pl.BlockSpec(memory_space=pltpu.SMEM)
+    anywhere = pl.BlockSpec(memory_space=pl.ANY)
+    dma = pltpu.SemaphoreType.DMA
+    return pl.pallas_call(
+        functools.partial(fused, count // LINE),
+        out_shape=jax.ShapeDtypeStruct((tok, width), jnp.bfloat16),
+        in_specs=[smem] * 3
+        + [anywhere, pl.BlockSpec(memory_space=pltpu.VMEM)]
+        + [anywhere] * 4,
+        out_specs=anywhere,
+        scratch_shapes=[
+            pltpu.VMEM((CHUNKS, count * rows, half // CHUNKS), jnp.bfloat16),
+            pltpu.VMEM((tok, columns), jnp.bfloat16),
+            pltpu.VMEM((2 * tok, columns), jnp.bfloat16),
+            pltpu.VMEM((2 * tok, columns), jnp.bfloat16),
+            pltpu.VMEM((2 * tok, columns), jnp.bfloat16),
+            pltpu.VMEM((2 * tok, half), jnp.bfloat16),
+            pltpu.VMEM((CHUNKS, 2 * tok, half // CHUNKS), jnp.bfloat16),
+            pltpu.VMEM((tok, 2 * tok), jnp.float32),
+            dma((4,)),
+            dma((CHUNKS,)),
+            dma((4,)),
+            dma((4,)),
+            dma((CHUNKS, count, 4)),
+            dma((CHUNKS, count)),
+            dma((CHUNKS,)),
+            dma((CHUNKS,)),
+            dma((CHUNKS,)),
+        ],
+        compiler_params=pltpu.CompilerParams(
+            collective_id=0, has_side_effects=True, vmem_limit_bytes=60 * 1024 * 1024
+        ),
+    )(
+        active_list,
+        active_count,
+        key_list,
+        block_input,
+        gate[None, :],
+        q_fresh,
+        resident[:, 0],
+        resident[:, 1],
+        out_weight,
+    )
+
+
+def per_device(groups, count, cores, *args):
+    rows, width = args[-1].shape
+    fits = groups == 2 and cores == 2 and count % LINE == 0 and rows % 16 == 0
+    fits = fits and width % (2 * CHUNKS * 128) == 0 and count * rows * width < 1 << 24
+    return local_fused(count, *args) if fits else local(*args)
+
 
 def solution(mesh):
     in_specs = (
@@ -146,5 +542,7 @@
         P(("groups", "fsdp"), None, None),
         P("fsdp", None),
     )
+    sizes = [mesh.shape[axis] for axis in ("groups", "fsdp", "blk")]
+    body = functools.partial(per_device, *sizes)
     out_specs = P(("groups", "fsdp", "blk"), None)
-    return jax.shard_map(local, mesh=mesh, in_specs=in_specs, out_specs=out_specs, check_vma=False)
+    return jax.shard_map(body, mesh=mesh, in_specs=in_specs, out_specs=out_specs, check_vma=False)

time: 246 us -> 126 us (0.51)
  waiting for transfers between devices: 129 us -> 0 us
  Pallas kernels: 0 us -> 112 us
  local copies, waits for them, and re-layouts: 37.8 us -> 8.26 us
  matrix products: 27.3 us -> 0 us
  other arithmetic: 26.2 us -> 5.29 us
  between operations: 13.5 us -> 0.03 us
  loops' own time: 9.54 us -> 0 us
    all_gather x1 -> x0, waiting for transfers between devices: 126 us -> none  [local(): half_weight = lax.all_gather(own_cols, 'fsdp', axis=0, tiled=True)]
    pallas_call x0 -> x1, Pallas kernels: none -> 112 us  [local_fused(): pl.pallas_call(functools.partial(fused, count // LINE), out_shape=jax.Sha...]
    dot_general x6 -> x0, matrix products: 27.3 us -> none  [the longest x2 8.35 us: block_partial(): jnp.einsum('hqk,khd->hqd', weights, value3, preferred_element_type=jnp.fl...]
    unnamed x19 -> x4, local copies, waits for them, and re-layouts: 17.4 us -> 4.06 us
    another operation x2 -> x0, loops' own time: 9.54 us -> none  [attend_block(): return lax.fori_loop(0, tile_count, one_slot, init_state)]
    select_n x6 -> x2, other arithmetic: 11.8 us -> 3.18 us  [the longest x1 3.17 us: local_fused(): resident = jnp.where(row_flags[:, None, None], kv_fresh, kv_cache)]
    slice x2 -> x0, local copies, waits for them, and re-layouts: 6.83 us -> none  [the longest x1 3.43 us: local(): other_kv[:, 1]]
    dynamic_slice x6 -> x1, local copies, waits for them, and re-layouts: 6.41 us -> 1.24 us  [local_fused(): flags = tile_flags(active_list[0, own_side], active_count[0, own_side])]
  transfers between devices with their start and end apart: 4 -> 0, of which waited for: 2 -> 0; matrix products, arithmetic and copies ran while one was open for 22% -> 0% of each run, Pallas kernels for 0% -> 0%
where the time goes in v1:
time: 126 us; the launch traced here: 125 us
  Pallas kernels  112 us (89%)
  local copies, waits for them, and re-layouts  8.26 us (7%)
  other arithmetic  5.29 us (4%)
    pallas_call x1, Pallas kernels, local_fused(): pl.pallas_call(functools.partial(fused, count // LINE), out_shape=jax.Sha...  112 us
    unnamed x4, local copies, waits for them, and re-layouts  4.06 us
    select_n x1, other arithmetic, local_fused(): resident = jnp.where(row_flags[:, None, None], kv_fresh, kv_cache)  3.17 us

profile of v1, /device:TPU:0, one launch (start us, length us, event | category | flops | bytes accessed | tf_op | source)
XLA Modules:
  0.0 125.3 jit_solution(3371611317720944971)
XLA Ops:
  0.0 1.2 constant_dynamic-slice_fusion
  1.2 0.6 iota_compare_fusion
  1.9 0.7 dynamic-slice_bitcast_fusion
  2.6 0.1 and_reduce_fusion
  2.7 0.6 fusion.2
  3.3 1.4 %select_reduce_fusion = pred[256]{0:T(512)(128)(4,1)S(1)} fusion(pred[]{:T(512)} %bitcast.8, pred[]{:T(512)} %bitcast.7, s32[256,1]{0,1:T(1,128)S(1)} %bitcast.18, s32[256,1]{0,1:T(1,128)S(1)} %bitcast.17), kind=kLoop, calls=%fused_computation.4 | loop fusion | flops 1024 | bytes 2306 | tf_op jit(solution)/shard_map/jit(_take)/gather | solution.py:476
  4.7 3.2 %copy_select_fusion = bf16[256,2,2560]{2,0,1:T(8,128)(2,1)S(1)} fusion(bf16[256,2,2560]{2,1,0:T(2,128)(2,1)} %param.15, bf16[256,2,2560]{2,1,0:T(2,128)(2,1)} %param.14, pred[256]{0:T(512)(128)(4,1)S(1)} %and_select_fusion), kind=kLoop, calls=%fused_computation | loop fusion | flops 1310720 | bytes 7864576 | tf_op jit(solution)/shard_map/jit(_where)/select_n | solution.py:477
  7.8 0.0 copy-start
  7.8 1.7 %slice_bitcast_fusion = (bf16[256,2560]{1,0:T(8,128)(2,1)}, bf16[256,2560]{1,0:T(8,128)(2,1)}) fusion(bf16[256,2,2560]{2,0,1:T(8,128)(2,1)S(1)} %copy_select_fusion), kind=kLoop, calls=%fused_computation.1 | loop fusion | bytes 5242880 | tf_op jit(solution)/shard_map/squeeze | solution.py:521
  9.5 0.0 copy-done
  9.5 0.7 copy.15.key_list
  10.2 111.7 %shard_map.91 = bf16[256,5120]{1,0:T(8,128)(2,1)} custom-call(s32[1,2,2]{2,1,0:T(2,128)} %active_list.1, s32[1,2]{1,0:T(1,128)} %active_count.1, s32[1,4,3]{2,1,0:T(4,128)} %copy.15.key_list, bf16[256,5120]{1,0:T(8,128)(2,1)} %block_hbm.1, f32[1,5120]{1,0:T(1,128)} %bitcast.16, bf16[256,2560]{1,0:T(8,128)(2,1)} %q_hbm.1, ...), custom_call_target="tpu_custom_call" | custom-call | tf_op jit(solution)/shard_map/pallas_call | solution.py:484
  121.9 3.4 %copy.19 = bf16[256,5120]{1,0:T(8,128)(2,1)} copy(bf16[256,5120]{1,0:T(8,128)(2,1)} %shard_map.91) | data formatting | bytes 5242880
  (3 shorter events, 0.0 us)
Async XLA Ops:
  7.8 1.7 %copy-start = (s32[1,4,3]{1,0,2:T(1,128)S(1)}, s32[1,4,3]{1,0,2:T(1,128)}, u32[]{:S(2)}) copy-start(s32[1,4,3]{1,0,2:T(1,128)} %param.18) | copy-start | bytes 148

commit v2 on v1

--- a/solution.py
+++ b/solution.py
@@ -149,12 +149,15 @@
     block_hbm,
     gate_ref,
     q_hbm,
-    k_hbm,
-    v_hbm,
+    fresh_hbm,
+    cache_hbm,
     w_hbm,
     out_hbm,
     weight,
     queries,
+    fresh,
+    cache,
+    wide,
     keys,
     values,
     attended,
@@ -227,8 +230,8 @@
 
     loads = [
         pltpu.make_async_copy(q_hbm, queries, load_sem.at[0]),
-        pltpu.make_async_copy(k_hbm, keys.at[pl.ds(0, tok)], load_sem.at[1]),
-        pltpu.make_async_copy(v_hbm, values.at[pl.ds(0, tok)], load_sem.at[2]),
+        pltpu.make_async_copy(fresh_hbm, fresh.at[pl.ds(0, tok)], load_sem.at[1]),
+        pltpu.make_async_copy(cache_hbm, cache.at[pl.ds(0, tok)], load_sem.at[2]),
         pltpu.make_async_copy(
             block_hbm.at[:, pl.ds(mine, half)], mixed_in.at[pl.ds(0, tok)], load_sem.at[3]
         ),
@@ -249,8 +252,8 @@
         )
 
     swaps = [
-        to_core(k_hbm, keys.at[pl.ds(tok, tok)], 0),
-        to_core(v_hbm, values.at[pl.ds(tok, tok)], 1),
+        to_core(fresh_hbm, fresh.at[pl.ds(tok, tok)], 0),
+        to_core(cache_hbm, cache.at[pl.ds(tok, tok)], 1),
         to_core(block_hbm.at[:, pl.ds(theirs, half)], mixed_in.at[pl.ds(tok, tok)], 2),
     ]
     give = to_core(attended.at[pl.ds(0, tok)], attended.at[pl.ds(tok, tok)], 3)
@@ -328,18 +331,41 @@
     step_x(0)
     pl.loop(1, 7)(lambda i: step_z(i, 0))
 
+    def is_active(side, a):
+        found = jnp.int32(0)
+        for slot in range(tiles):
+            hit = (active_list[0, side, slot] == a) & (slot < active_count[0, side])
+            found = jnp.where(hit, jnp.int32(1), found)
+        return found
+
+    flags = [is_active(side, a) for side in (b, 1 - b) for a in range(tiles)]
+
+    def settle(side, h):
+        cols = pl.ds(pl.multiple_of(h * HEAD_DIM, 128), HEAD_DIM)
+        for a in range(tiles):
+            place = side * tiles + a
+            span = pl.ds(place * tile_rows, tile_rows)
+            pair = jnp.where(flags[place] > 0, fresh[span, :, cols], cache[span, :, cols])
+            pair = pair.reshape(2 * tile_rows, HEAD_DIM)
+            wide[pl.ds(2 * a * tile_rows, 2 * tile_rows), :] = pair.astype(jnp.float32)
+        whole = pl.ds(side * tok, tok)
+        keys[whole, cols] = wide[pl.ds(0, tok, 2), :].astype(jnp.bfloat16)
+        values[whole, cols] = wide[pl.ds(1, tok, 2), :].astype(jnp.bfloat16)
+
     for load in loads[:3]:
         load.wait()
+    pl.loop(0, heads)(functools.partial(settle, 0))
     for swap in swaps[:2]:
         swap.wait_recv()
+    pl.loop(0, heads)(functools.partial(settle, 1))
 
     for a in range(tiles):
         for t in range(2 * tiles):
             side = b if t < tiles else 1 - b
             tile_id = side * tiles + t % tiles
             listed = jnp.int32(0)
-            for slot in range(key_list.shape[2]):
-                hit = key_list[0, b * tiles + a, slot] == tile_id
+            for slot in range(key_list.shape[0]):
+                hit = key_list[slot, 0, b * tiles + a] == tile_id
                 listed = jnp.where(hit, jnp.int32(1), listed)
             mask[pl.ds(a * tile_rows, tile_rows), pl.ds(t * tile_rows, tile_rows)] = jnp.full(
                 (tile_rows, tile_rows), listed.astype(jnp.float32), jnp.float32
@@ -396,15 +422,6 @@
     swaps[2].wait_recv()
     give.wait_recv()
 
-    def is_active(side, a):
-        found = jnp.int32(0)
-        for slot in range(tiles):
-            hit = (active_list[0, side, slot] == a) & (slot < active_count[0, side])
-            found = jnp.where(hit, jnp.int32(1), found)
-        return found
-
-    flags = [is_active(side, a) for side in (b, 1 - b) for a in range(tiles)]
-
     def out_copies(c):
         cols = pl.ds(pl.multiple_of(mine + c * width, 128), width)
         return (
@@ -470,16 +487,11 @@
     count, block_input, gate, q_fresh, kv_fresh, kv_cache, active_list, active_count, key_list, out_weight
 ):
     tok, width = block_input.shape
-    own_side = lax.axis_index("blk")
-    tiles = active_list.shape[2]
-    flags = tile_flags(active_list[0, own_side], active_count[0, own_side])
-    row_flags = jnp.repeat(flags, tok // tiles, total_repeat_length=tok)
-    resident = jnp.where(row_flags[:, None, None], kv_fresh, kv_cache)
     rows = out_weight.shape[0]
     half = width // 2
     columns = q_fresh.shape[1]
     smem = pl.BlockSpec(memory_space=pltpu.SMEM)
-    anywhere = pl.BlockSpec(memory_space=pl.ANY)
+    anywhere = pl.BlockSpec(memory_space=pltpu.HBM)
     dma = pltpu.SemaphoreType.DMA
     return pl.pallas_call(
         functools.partial(fused, count // LINE),
@@ -487,10 +499,13 @@
         in_specs=[smem] * 3
         + [anywhere, pl.BlockSpec(memory_space=pltpu.VMEM)]
         + [anywhere] * 4,
-        out_specs=anywhere,
+        out_specs=pl.BlockSpec(memory_space=pl.ANY),
         scratch_shapes=[
             pltpu.VMEM((CHUNKS, count * rows, half // CHUNKS), jnp.bfloat16),
             pltpu.VMEM((tok, columns), jnp.bfloat16),
+            pltpu.VMEM((2 * tok, 2, columns), jnp.bfloat16),
+            pltpu.VMEM((2 * tok, 2, columns), jnp.bfloat16),
+            pltpu.VMEM((2 * tok, HEAD_DIM), jnp.float32),
             pltpu.VMEM((2 * tok, columns), jnp.bfloat16),
             pltpu.VMEM((2 * tok, columns), jnp.bfloat16),
             pltpu.VMEM((2 * tok, columns), jnp.bfloat16),
@@ -508,17 +523,17 @@
             dma((CHUNKS,)),
         ],
         compiler_params=pltpu.CompilerParams(
-            collective_id=0, has_side_effects=True, vmem_limit_bytes=60 * 1024 * 1024
+            collective_id=0, has_side_effects=True, vmem_limit_bytes=60000000
         ),
     )(
         active_list,
         active_count,
-        key_list,
+        key_list.transpose(2, 0, 1),
         block_input,
         gate[None, :],
         q_fresh,
-        resident[:, 0],
-        resident[:, 1],
+        kv_fresh,
+        kv_cache,
         out_weight,
     )
 

time: 126 us -> 115 us (0.913)
  other arithmetic: 5.29 us -> 0 us
  local copies, waits for them, and re-layouts: 8.26 us -> 3.4 us
    select_n x2 -> x0, other arithmetic: 3.18 us -> none  [the longest x1 3.17 us: local_fused(): resident = jnp.where(row_flags[:, None, None], kv_fresh, kv_cache)]
    squeeze x1 -> x0, local copies, waits for them, and re-layouts: 1.69 us -> none  [local_fused(): resident[:, 1]]
    gather x1 -> x0, other arithmetic: 1.36 us -> none  [local_fused(): row_flags = jnp.repeat(flags, tok // tiles, total_repeat_length=tok)]
    unnamed x4 -> x1, local copies, waits for them, and re-layouts: 4.06 us -> 3.4 us
where the time goes in v2:
time: 115 us
  Pallas kernels  112 us (97%)
  local copies, waits for them, and re-layouts  3.4 us (3%)
    pallas_call x1, Pallas kernels, local_fused(): pl.pallas_call(functools.partial(fused, count // LINE), out_shape=jax.Sha...  112 us
    unnamed x1, local copies, waits for them, and re-layouts  3.4 us

profile of v2, /device:TPU:0, one launch (start us, length us, event | category | flops | bytes accessed | tf_op | source)
XLA Modules:
  0.0 115.1 jit_solution(8150992041843743909)
XLA Ops:
  0.0 111.7 %shard_map.91 = bf16[256,5120]{1,0:T(8,128)(2,1)} custom-call(s32[1,2,2]{2,1,0:T(2,128)} %active_list.1, s32[1,2]{1,0:T(1,128)} %active_count.1, s32[3,1,4]{2,1,0:T(1,128)} %bitcast.3, bf16[256,5120]{1,0:T(8,128)(2,1)} %block_hbm.1, f32[1,5120]{1,0:T(1,128)} %bitcast.2, bf16[256,2560]{1,0:T(8,128)(2,1)} %q_hbm.1, bf16[256,2,2560]{2,1,0:T(2,128)(2,1)} %fresh_hbm.1, ...), custom_call_target="tpu_custom_call" | custom-call | tf_op jit(solution)/shard_map/pallas_call | solution.py:496
  111.7 3.4 %copy.11 = bf16[256,5120]{1,0:T(8,128)(2,1)} copy(bf16[256,5120]{1,0:T(8,128)(2,1)} %shard_map.91) | data formatting | bytes 5242880

commit v3 on v2

--- a/solution.py
+++ b/solution.py
@@ -137,7 +137,11 @@
     return jnp.where(row_flags[:, None], mixed.astype(jnp.bfloat16), block_input)
 
 MESH = pl.DeviceIdType.MESH
-CHUNKS = 10
+CHUNKS = 20
+TURNED = 2
+SHARED = 4
+HELD = TURNED + SHARED
+STREAMS = CHUNKS - HELD
 LINE = 2
 
 
@@ -216,14 +220,14 @@
             w_sem.at[c],
         )
 
+    def held(i, owner):
+        return jnp.where(i < TURNED, owner * TURNED + i, TURNED + owner * SHARED + i)
+
     def stream(i):
-        return jnp.where(i == 0, y, jnp.where(i < 3, 1 + 2 * y + i, 3 + i))
-
-    def passive(i):
-        return jnp.where(i == 0, 1 - y, 3 - 2 * y + i)
+        return jnp.where(i < HELD, held(i, y), HELD + i)
 
     def every(i):
-        return jnp.where(i < 7, stream(i), passive(i - 7))
+        return jnp.where(i < STREAMS, stream(i), held(i - STREAMS, 1 - y))
 
     for i in range(CHUNKS):
         own_weight(every(jnp.int32(i))).start()
@@ -320,16 +324,19 @@
 
     levels = depth + LINE - 1
 
-    def step_x(level, done=False):
+    def step_x(i, level, done=False):
         for dz, dx in offsets(level):
-            visit(y, "x", True, dz, dx, done)
+            visit(stream(i), "x", True, dz, dx, done)
 
     def step_z(i, level, done=False):
         for dz, dx in offsets(level):
-            visit(stream(i), "z", i < 3, dz, dx, done)
-
-    step_x(0)
-    pl.loop(1, 7)(lambda i: step_z(i, 0))
+            visit(stream(i), "z", i < HELD, dz, dx, done)
+
+    def all_steps(level, done=False):
+        pl.loop(0, TURNED)(functools.partial(step_x, level=level, done=done))
+        pl.loop(TURNED, STREAMS)(functools.partial(step_z, level=level, done=done))
+
+    all_steps(0)
 
     def is_active(side, a):
         found = jnp.int32(0)
@@ -403,20 +410,18 @@
     def attend_range(low, high):
         pl.loop(low, high)(attend)
 
-    each = heads // 7
-    first = heads - 6 * each
-    step_x(1)
-    attend_range(0, first)
-
-    @pl.loop(1, 7)
+    each = -(-heads // (STREAMS - TURNED))
+    pl.loop(0, TURNED)(functools.partial(step_x, level=1))
+
+    @pl.loop(TURNED, STREAMS)
     def _(i):
         step_z(i, 1)
-        attend_range(first + (i - 1) * each, first + i * each)
+        low = (i - TURNED) * each
+        attend_range(jnp.minimum(low, heads), jnp.minimum(low + each, heads))
 
     give.start()
     for level in range(2, levels - 1):
-        step_x(level)
-        pl.loop(1, 7)(functools.partial(step_z, level=level))
+        all_steps(level)
 
     loads[3].wait()
     swaps[2].wait_recv()
@@ -439,18 +444,21 @@
         )
 
     def project(j):
-        i = jnp.where(j < 3, j, jnp.where(j < 6, j + 4, j - 3))
+        t = j - HELD
+        i = jnp.where(t % 2 == 0, HELD + t // 2, STREAMS + t // 2)
+        i = jnp.where(t < 2 * HELD, i, t)
+        i = jnp.where(t < 0, j, i)
         c = every(i)
 
-        @pl.when(j == 0)
+        @pl.when(i < TURNED)
         def _():
-            step_x(levels - 1)
-
-        @pl.when((j == 1) | (j == 2) | (j >= 6))
+            step_x(i, levels - 1)
+
+        @pl.when((i >= TURNED) & (i < STREAMS))
         def _():
             step_z(i, levels - 1)
 
-        @pl.when((j >= 3) & (j < 6))
+        @pl.when(i >= STREAMS)
         def _():
             own_weight(c).wait()
             for s in range(depth * LINE):
@@ -473,8 +481,7 @@
     for swap in swaps + [give]:
         swap.wait_send()
     for level in range(levels):
-        step_x(level, done=True)
-        pl.loop(1, 7)(functools.partial(step_z, level=level, done=True))
+        all_steps(level, done=True)
 
     @pl.loop(0, CHUNKS)
     def _(c):

time: 115 us -> 124 us (1.078)
  the two profiles are of different devices: /device:TPU:0 before, /device:TPU:8 now
where the time goes in v3:
time: 124 us
  Pallas kernels  121 us (98%)
  local copies, waits for them, and re-layouts  3.4 us (3%)
    pallas_call x1, Pallas kernels, local_fused(): pl.pallas_call(functools.partial(fused, count // LINE), out_shape=jax.Sha...  121 us
    unnamed x1, local copies, waits for them, and re-layouts  3.4 us

profile of v3, /device:TPU:8, one launch (start us, length us, event | category | flops | bytes accessed | tf_op | source)
XLA Modules:
  0.0 124.2 jit_solution(10312821279922821332)
XLA Ops:
  0.0 120.8 %shard_map.91 = bf16[256,5120]{1,0:T(8,128)(2,1)} custom-call(s32[1,2,2]{2,1,0:T(2,128)} %active_list.1, s32[1,2]{1,0:T(1,128)} %active_count.1, s32[3,1,4]{2,1,0:T(1,128)} %bitcast.3, bf16[256,5120]{1,0:T(8,128)(2,1)} %block_hbm.1, f32[1,5120]{1,0:T(1,128)} %bitcast.2, bf16[256,2560]{1,0:T(8,128)(2,1)} %q_hbm.1, bf16[256,2,2560]{2,1,0:T(2,128)(2,1)} %fresh_hbm.1, ...), custom_call_target="tpu_custom_call" | custom-call | tf_op jit(solution)/shard_map/pallas_call | solution.py:503
  120.8 3.4 %copy.11 = bf16[256,5120]{1,0:T(8,128)(2,1)} copy(bf16[256,5120]{1,0:T(8,128)(2,1)} %shard_map.91) | data formatting | bytes 5242880
